TPU v7x, 32 devices: a whole 2x2x4 slice. The times are simulated.
32 devices in a mesh: row: 8 (over z, y), col: 4 (over x, core).
Axes of the slice: x: 2, y: 2, z: 4, core: 2. Of those that a mesh axis runs over, the one named last changes fastest.
Arguments:
- points: float32 [8, 5120], P(None, ('row', 'col')), may hold values from -6 to 6
- sketch: bfloat16 [5120, 256], P(('row', 'col')), may hold values from -0.625 to 0.625
- rank: int32 [5120], P(('row', 'col')), may hold values from 0 to 5119, each once
- boundary: int32 [1], replicated, may hold values from 1280 to 3840
- scales: float32 [8], replicated, may hold values from 1.5 to 4
Outputs:
- basis: float32 [5120, 256], P(('row', 'col'))
- factor: float32 [256, 256], replicated
Inputs may be any that keep to these rules, and one draw needn't show every extreme that they name: `rank`: each tree position appears once.
All inputs are finite; a program needn't handle non-finite values.
Results may differ from a plain program's by a relative error of at most 0.0006.
The roundings to bfloat16 on the way count: a program that leaves them out, or rounds other values in their place, can miss the bound.
Values may be sent and summed in bfloat16 or wider, within the bound.
A program may use at most 64 MiB of HBM per device.

v0:
```python
import functools

import jax
import jax.numpy as jnp
from jax import lax
from jax.experimental import pallas as pl
from jax.experimental.pallas import tpu as pltpu
from jax.sharding import PartitionSpec as P

HIGHEST = lax.Precision.HIGHEST
FAR = 5000.0
VMEM = pl.BlockSpec(memory_space=pltpu.VMEM)
SMEM = pl.BlockSpec(memory_space=pltpu.SMEM)


def dot(a, b, dims, precision=HIGHEST):
    return lax.dot_general(
        a, b, (dims, ((), ())), precision=precision, preferred_element_type=jnp.float32
    )


def remote(src, dst, send, recv, row, col):
    return pltpu.make_async_remote_copy(
        src_ref=src,
        dst_ref=dst,
        send_sem=send,
        recv_sem=recv,
        device_id=(row, col),
        device_id_type=pl.DeviceIdType.MESH,
    )


def each(start, stop, step):
    def run(index, carry):
        step(index)
        return carry

    lax.fori_loop(start, stop, run, 0)


def tile_kernel(
    rows, cols, points, tests, rank, boundary, scales, out, info, srcs, tgts, bank, left,
    s_tgt, r_tgt, s_along, r_along, s_info, r_info, s_over, r_over, s_mate, r_mate,
):
    row, col = lax.axis_index("row"), lax.axis_index("col")
    lines = rows // 2
    line, odd = row // 2, row % 2
    mate = row + 1 - 2 * odd
    local = tests.shape[0]

    def at(k):
        return 2 * ((line + k) % lines) + odd

    def origin(k):
        return 2 * ((line + lines - k) % lines) + odd

    barrier = pltpu.get_barrier_semaphore()
    mesh = pl.DeviceIdType.MESH
    each(1, cols, lambda k: pl.semaphore_signal(barrier, 1, device_id=(row, (col + k) % cols), device_id_type=mesh))
    each(1, lines, lambda k: pl.semaphore_signal(barrier, 1, device_id=(at(k), col), device_id_type=mesh))
    pl.semaphore_signal(barrier, 1, device_id=(mate, col), device_id_type=mesh)
    sq = points.shape[0]
    spot = lax.broadcasted_iota(jnp.int32, points.shape, 0)
    scale = jnp.ones(points.shape, jnp.float32)
    for i in range(sq):
        scale = jnp.where(spot == i, scales[i], scale)
    scaled = points[...] / scale
    side = jnp.where(rank[...] >= boundary[0], 1.0, 0.0)
    own = jnp.concatenate(
        [
            scaled,
            -0.5 * jnp.sum(scaled * scaled, axis=0, keepdims=True),
            jnp.ones_like(side),
            side,
            1.0 - side,
            jnp.zeros((info.shape[0] - sq - 4, local), jnp.float32),
        ],
        axis=0,
    )
    info[...] = own
    srcs[row] = own
    tgts[col] = own
    bank[row] = tests[...]
    pl.semaphore_wait(barrier, cols + lines - 1)

    def tgt(k):
        return remote(info, tgts.at[col], s_tgt.at[k], r_tgt.at[k], row, (col + k) % cols)

    def along(k):
        return (
            remote(info, srcs.at[row], s_info.at[k], r_info.at[k], at(k), col),
            remote(tests, bank.at[row], s_along.at[k], r_along.at[k], at(k), col),
        )

    def over(k):
        place = origin(k)
        return (
            remote(srcs.at[place], srcs.at[place], s_mate.at[k], r_mate.at[k], mate, col),
            remote(bank.at[place], bank.at[place], s_over.at[k], r_over.at[k], mate, col),
        )

    def first():
        return (
            remote(info, srcs.at[row], s_mate.at[0], r_mate.at[0], mate, col),
            remote(tests, bank.at[row], s_over.at[0], r_over.at[0], mate, col),
        )

    def go(copies):
        for copy in copies:
            copy.start()

    def come(copies):
        for copy in copies:
            copy.wait_recv()

    def leave(copies):
        for copy in copies:
            copy.wait_send()

    each(1, cols, lambda k: tgt(k).start())
    go(first())
    each(1, lines, lambda k: go(along(k)))
    each(1, cols, lambda k: tgt(k).wait())
    for place in range(cols):
        block = tgts[2 * (place % (cols // 2)) + place // (cols // 2)]
        half, one = block[sq : sq + 1], block[sq + 1 : sq + 2]
        side, other = block[sq + 2 : sq + 3], block[sq + 3 : sq + 4]
        left[place * local : (place + 1) * local, :] = jnp.concatenate(
            [block[:sq], one, half, -FAR * side, -FAR * other, block[sq + 4 :]], axis=0
        ).T
    step = 2 * local

    def add(place, fresh=False):
        source, test = srcs[place], bank[place]

        def chunk(index):
            rows_of = pl.ds(pl.multiple_of(index * step, step), step)
            power = dot(left[rows_of, :], source, ((1,), (0,)))
            tile = jnp.exp(power).astype(jnp.bfloat16)
            term = dot(tile, test, ((1,), (0,)), None)
            out[rows_of, :] = term if fresh else out[rows_of, :] + term

        each(0, cols // 2, chunk)

    add(row, True)

    def turn(k):
        come(along(k))
        go(over(k))
        add(origin(k))
        come(over(k - 1))
        add(origin(k - 1) + 1 - 2 * odd)

    each(1, lines, turn)
    come(over(lines - 1))
    add(origin(lines - 1) + 1 - 2 * odd)
    leave(first())
    each(1, lines, lambda k: leave(along(k) + over(k)))


def tiles(points, tests, rank, boundary, scales, rows, cols):
    depth, local = 8 * ((points.shape[0] + 11) // 8), points.shape[1]
    ranks = tests.shape[1]
    lines = rows // 2
    dma = pltpu.SemaphoreType.DMA
    return pl.pallas_call(
        functools.partial(tile_kernel, rows, cols),
        out_shape=jax.ShapeDtypeStruct((cols * local, ranks), jnp.float32),
        in_specs=[VMEM, VMEM, VMEM, SMEM, SMEM],
        out_specs=VMEM,
        scratch_shapes=[
            pltpu.VMEM((depth, local), jnp.float32),
            pltpu.VMEM((rows, depth, local), jnp.float32),
            pltpu.VMEM((cols, depth, local), jnp.float32),
            pltpu.VMEM((rows, local, ranks), tests.dtype),
            pltpu.VMEM((cols * local, depth), jnp.float32),
            dma((cols,)), dma((cols,)),
            dma((lines,)), dma((lines,)), dma((lines,)), dma((lines,)),
            dma((lines,)), dma((lines,)), dma((lines,)), dma((lines,)),
        ],
        compiler_params=pltpu.CompilerParams(collective_id=0, has_side_effects=True),
        name="tiles",
    )(points, tests, rank[None], boundary, scales)


def reduce_kernel(
    rows, cols, part, sample, gram, pair, stage, far, square, mate, mine, piece, done,
    s_pair, r_pair, s_far, r_far, s_mate, r_mate, s_piece, r_piece, s_done, r_done, s_over, r_over,
):
    row, col = lax.axis_index("row"), lax.axis_index("col")
    half = cols // 2
    count = rows * half
    parity, spot = col % 2, col // 2
    partner = col + 1 - 2 * parity
    index = row * half + spot

    def place(i):
        return i // half, 2 * (i % half) + parity

    barrier = pltpu.get_barrier_semaphore()
    pl.semaphore_signal(barrier, 1, device_id=(row, partner), device_id_type=pl.DeviceIdType.MESH)
    each(1, count, lambda k: pl.semaphore_signal(barrier, 1, device_id=place((index + k) % count), device_id_type=pl.DeviceIdType.MESH))
    pl.semaphore_wait(barrier, count)

    def swap(k):
        there = (spot + k) % half
        return remote(part.at[1 - parity, there], pair.at[there], s_pair.at[k], r_pair.at[k], row, partner)

    def send(k):
        there = (spot + k) % half
        return remote(stage.at[there], far.at[k], s_far.at[k], r_far.at[k], row, 2 * there + parity)

    def merge(k):
        there = (spot + k) % half
        swap(k).wait()
        stage[there] = part[parity, there] + pair[there]

    def forward(k):
        merge(k)
        send(k).start()

    each(1, half, lambda k: swap(k).start())
    swap(0).start()
    each(1, half, forward)
    merge(0)
    each(1, half, lambda k: send(k).wait())
    total = stage[spot]
    for k in range(1, half):
        total = total + far[k]
    sample[...] = total

    square[...] = dot(total.T, total, ((1,), (0,))).reshape(square.shape)
    trade = remote(square.at[1 - parity], mate, s_mate.at[0], r_mate.at[0], row, partner)
    trade.start()
    trade.wait()
    mine[...] = square[parity] + mate[...]

    def scatter(k):
        there = (index + k) % count
        r, c = place(there)
        return remote(mine.at[there], piece.at[k], s_piece.at[k], r_piece.at[k], r, c)

    each(1, count, lambda k: scatter(k).start())
    each(1, count, lambda k: scatter(k).wait())
    piece[0] = mine[index]
    done[...] = jnp.sum(piece[...], axis=0)
    gram[parity, index] = done[...]

    def collect(k):
        r, c = place((index + k) % count)
        return remote(done, gram.at[parity, index], s_done.at[k], r_done.at[k], r, c)

    def pass_on(k):
        there = (index + count - k) % count
        return remote(gram.at[parity, there], gram.at[parity, there], s_over.at[k], r_over.at[k], row, partner)

    def relay(k):
        collect(k).wait_recv()
        pass_on(k).start()

    own = remote(done, gram.at[parity, index], s_over.at[0], r_over.at[0], row, partner)
    each(1, count, lambda k: collect(k).start())
    own.start()
    each(1, count, relay)
    own.wait()
    each(1, count, lambda k: pass_on(k).wait())
    each(1, count, lambda k: collect(k).wait_send())


def reduce(part, rows, cols):
    local, ranks = part.shape[0] // cols, part.shape[1]
    half, count = cols // 2, rows * cols // 2
    share = ranks // 2 // count
    f32 = jnp.float32
    dma = pltpu.SemaphoreType.DMA
    sample, gram = pl.pallas_call(
        functools.partial(reduce_kernel, rows, cols),
        out_shape=(
            jax.ShapeDtypeStruct((local, ranks), f32),
            jax.ShapeDtypeStruct((2, count, share, ranks), f32),
        ),
        in_specs=[VMEM],
        out_specs=(VMEM, VMEM),
        scratch_shapes=[
            pltpu.VMEM((half, local, ranks), f32),
            pltpu.VMEM((half, local, ranks), f32),
            pltpu.VMEM((half, local, ranks), f32),
            pltpu.VMEM((2, count, share, ranks), f32),
            pltpu.VMEM((count, share, ranks), f32),
            pltpu.VMEM((count, share, ranks), f32),
            pltpu.VMEM((count, share, ranks), f32),
            pltpu.VMEM((share, ranks), f32),
            dma((half,)), dma((half,)), dma((half,)), dma((half,)), dma((1,)), dma((1,)), dma((count,)), dma((count,)), dma((count,)), dma((count,)), dma((count,)), dma((count,)),
        ],
        compiler_params=pltpu.CompilerParams(collective_id=1, has_side_effects=True),
        name="reduce",
    )(part.reshape(2, half, local, ranks))
    return sample, gram.reshape(ranks, ranks)


def factor_block(a):
    size, wide = a.shape[0], 8
    shape = (wide, size)
    lane = lax.broadcasted_iota(jnp.int32, shape, 1)
    line = lax.broadcasted_iota(jnp.int32, shape, 0)

    def spread(x):
        return jnp.broadcast_to(x, shape)

    blocks = [a[i : i + wide] for i in range(0, size, wide)]
    upper, inverse = [], []
    for b in range(size // wide):
        at = b * wide
        inside = (lane >= at) & (lane < at + wide)
        x = blocks[b]
        y = jnp.where(inside, jnp.where(lane - at == line, 1.0, 0.0), x)
        marks = [spread(x[:, at + u : at + u + 1]) for u in range(wide)]
        over, root = jnp.zeros(shape, jnp.float32), jnp.zeros(shape, jnp.float32)
        for s in range(wide):
            pivot = spread(marks[s][s : s + 1])
            inv = 1.0 / pivot
            over = jnp.where(line == s, inv, over)
            root = jnp.where(line == s, pivot, root)
            if s + 1 < wide:
                low = jnp.where(line > s, marks[s] * inv, 0.0)
                for u in range(s + 1, wide):
                    marks[u] = marks[u] - low * spread(marks[u][s : s + 1])
                x = x - low * spread(x[s : s + 1])
                y = y - low * spread(y[s : s + 1])
        z = y * over
        for s in range(wide - 1, 0, -1):
            z = z - jnp.where(line < s, marks[s] * over, 0.0) * spread(z[s : s + 1])
        rows = [spread(z[t : t + 1]) for t in range(wide)]
        for i in range(b + 1, size // wide):
            old = blocks[i]
            parts = [spread(old[:, at + t : at + t + 1]) * rows[t] for t in range(wide)]
            while len(parts) > 1:
                parts = [p + q for p, q in zip(parts[::2], parts[1::2])]
            blocks[i] = jnp.where(inside, 0.0, old) - parts[0]
        root = lax.rsqrt(root)
        upper.append(jnp.where(lane >= at + line, x * root, 0.0))
        inverse.append(jnp.where(lane <= at + line, y * root, 0.0))
    return jnp.concatenate(upper, axis=0), jnp.concatenate(inverse, axis=0)


def finish_kernel(scale, gram, sample, basis, factor, up, low):
    ranks = gram.shape[0]
    half = ranks // 2
    mean = gram[...] * scale
    same = lax.broadcasted_iota(jnp.int32, (ranks, ranks), 0) == lax.broadcasted_iota(jnp.int32, (ranks, ranks), 1)
    trace = jnp.sum(jnp.sum(jnp.where(same, mean, 0.0), axis=1, keepdims=True), axis=0, keepdims=True)
    factor[...] = jnp.where(same, mean + (0.1 / ranks) * trace, mean)
    cross = factor[:half, half:]

    def one(index):
        start = pl.multiple_of(index * half, half)
        block = factor[pl.ds(start, half), pl.ds(start, half)]
        u, m = factor_block(block)
        up[index] = u
        low[index] = m

        @pl.when(index == 0)
        def _():
            lift = dot(m, cross, ((1,), (0,)))
            up[2] = lift
            factor[half:, half:] = factor[half:, half:] - dot(lift.T, lift, ((1,), (0,)))

    each(0, 2, one)
    lift = up[2]
    first = dot(sample[:, :half], low[0], ((1,), (1,)))
    second = dot(sample[:, half:] - dot(first, lift, ((1,), (0,))), low[1], ((1,), (1,)))
    basis[:, :half] = first
    basis[:, half:] = second
    factor[:half, :half] = up[0].T
    factor[:half, half:] = jnp.zeros((half, half), jnp.float32)
    factor[half:, :half] = lift.T
    factor[half:, half:] = up[1].T


def finish(gram, sample, everyone):
    ranks = gram.shape[0]
    half = ranks // 2
    return pl.pallas_call(
        functools.partial(finish_kernel, 1.0 / everyone),
        out_shape=(
            jax.ShapeDtypeStruct(sample.shape, jnp.float32),
            jax.ShapeDtypeStruct(gram.shape, jnp.float32),
        ),
        in_specs=[VMEM, VMEM],
        out_specs=(VMEM, VMEM),
        scratch_shapes=[pltpu.VMEM((3, half, half), jnp.float32), pltpu.VMEM((2, half, half), jnp.float32)],
        name="finish",
    )(gram, sample)


def body(rows, cols, points, sketch, rank, boundary, scales):
    sample, gram = reduce(tiles(points, sketch, rank, boundary, scales, rows, cols), rows, cols)
    return finish(gram, sample, rows * cols * points.shape[1])


def solution(mesh):
    placed = (P(None, ("row", "col")), P(("row", "col"), None), P(("row", "col")), P(), P())
    return jax.shard_map(
        functools.partial(body, mesh.shape["row"], mesh.shape["col"]),
        mesh=mesh,
        in_specs=placed,
        out_specs=(P(("row", "col"), None), P()),
        check_vma=False,
    )
```

profile of v0, /device:TPU:0, one launch (start us, length us, event | category | flops | bytes accessed | tf_op | source)
XLA Modules:
  0.0 66.2 jit_solution(3639975585981655172)
XLA Ops:
  1.3 23.3 %tiles.1 = f32[640,256]{1,0:T(8,128)} custom-call(f32[8,160]{1,0:T(8,128)} %points.1, bf16[160,256]{1,0:T(8,128)(2,1)} %tests.1, s32[1,160]{1,0:T(1,128)} %bitcast.5, s32[1]{0:T(128)S(6)} %copy.7.boundary, f32[8]{0:T(128)} %scales.1), custom_call_target="tpu_custom_call" | custom-call | tf_op jit(solution)/shard_map/tiles/pallas_call | solution.py:166
  24.6 27.9 %reduce.1 = (f32[160,256]{1,0:T(8,128)}, f32[2,16,8,256]{3,2,1,0:T(8,128)}) custom-call(f32[2,2,160,256]{3,2,1,0:T(8,128)} %bitcast.3), custom_call_target="tpu_custom_call" | custom-call | tf_op jit(solution)/shard_map/reduce/pallas_call | solution.py:276
  52.4 13.8 %finish.1 = (f32[160,256]{1,0:T(8,128)}, f32[256,256]{1,0:T(8,128)}) custom-call(f32[256,256]{1,0:T(8,128)} %bitcast.4, f32[160,256]{1,0:T(8,128)} %get-tuple-element.5.sample), custom_call_target="tpu_custom_call" | custom-call | tf_op jit(solution)/shard_map/finish/pallas_call | solution.py:383
where the time goes:
time: 66.4 us; the launch traced here: 66.2 us
  Pallas kernels  64.9 us (98%)
  between operations  1.29 us (2%)
    pallas_call x1, Pallas kernels, reduce(): pl.pallas_call(functools.partial(reduce_kernel, rows, cols), out_shape=(j...  27.9 us
    pallas_call x1, Pallas kernels, tiles(): pl.pallas_call(functools.partial(tile_kernel, rows, cols), out_shape=jax....  23.3 us
    pallas_call x1, Pallas kernels, finish(): pl.pallas_call(functools.partial(finish_kernel, 1.0 / everyone), out_shap...  13.8 us

commit v1 on v0

v1 whole, which is shorter than its diff:
```python
import functools

import jax
import jax.numpy as jnp
from jax import lax
from jax.experimental import pallas as pl
from jax.experimental.pallas import tpu as pltpu
from jax.sharding import PartitionSpec as P

HIGHEST = lax.Precision.HIGHEST
FAR = 4992.0
VMEM = pl.BlockSpec(memory_space=pltpu.VMEM)
SMEM = pl.BlockSpec(memory_space=pltpu.SMEM)


def dot(a, b, dims, precision=HIGHEST):
    return lax.dot_general(
        a, b, (dims, ((), ())), precision=precision, preferred_element_type=jnp.float32
    )


def remote(src, dst, send, recv, row, col):
    return pltpu.make_async_remote_copy(
        src_ref=src,
        dst_ref=dst,
        send_sem=send,
        recv_sem=recv,
        device_id=(row, col),
        device_id_type=pl.DeviceIdType.MESH,
    )


def each(start, stop, step):
    def run(index, carry):
        step(index)
        return carry

    lax.fori_loop(start, stop, run, 0)


def thirds(x):
    high = x.astype(jnp.bfloat16).astype(jnp.float32)
    mid = (x - high).astype(jnp.bfloat16).astype(jnp.float32)
    return high, mid, (x - high - mid).astype(jnp.bfloat16).astype(jnp.float32)


def sample_kernel(
    rows, cols, points, tests, rank, boundary, scales, sample, gram, front, back, left,
    square, mate, mine, piece, done,
    s_z, r_z, s_a, r_a, s_b, r_b, s_c, r_c,
    s_mate, r_mate, s_piece, r_piece, s_done, r_done, s_over, r_over,
):
    row, col = lax.axis_index("row"), lax.axis_index("col")
    lines, half = rows // 2, cols // 2
    line, odd = row // 2, row % 2
    spot, parity = col // 2, col % 2
    local = tests.shape[0]
    split = local - back.shape[-2]
    dims = points.shape[0]
    mesh = pl.DeviceIdType.MESH
    above, below = line < lines - 1, line > 0

    def there(l, o, s, p):
        return 2 * l + o, 2 * s + p

    barrier = pltpu.get_barrier_semaphore()

    def greet(l, o, s, p):
        pl.semaphore_signal(barrier, 1, device_id=there(l, o, s, p), device_id_type=mesh)

    @pl.when(above)
    def _():
        greet(line + 1, odd, spot, parity)

    @pl.when(below)
    def _():
        greet(line - 1, odd, spot, parity)

    for k in range(1, half):
        greet(line, odd, (spot + k) % half, parity)
    greet(line, 1 - odd, spot, parity)
    greet(line, odd, spot, 1 - parity)

    index = lax.broadcasted_iota(jnp.int32, points.shape, 0)
    scale = jnp.ones(points.shape, jnp.float32)
    for i in range(dims):
        scale = jnp.where(index == i, scales[i], scale)
    scaled = points[...] / scale
    side = jnp.where(rank[...] >= boundary[0], 1.0, 0.0)
    gap = jnp.zeros((-dims % 8, local), jnp.float32)
    high, mid, low = [jnp.concatenate([part, gap], axis=0) if dims % 8 else part for part in thirds(scaled)]
    norms = list(thirds(-0.5 * jnp.sum(scaled * scaled, axis=0, keepdims=True)))
    ones = [jnp.ones_like(side)] * 3
    info = jnp.concatenate([high, mid, low, side, 1.0 - side] + norms + ones, axis=0)
    wide = jnp.zeros((info.shape[0], tests.shape[1] - local), jnp.float32)
    front[line, odd, parity, spot, :split] = tests[:split]
    front[line, odd, parity, spot, split:] = jnp.concatenate([info, wide], axis=1).astype(jnp.bfloat16)
    back[line, spot, parity, odd] = tests[split:]
    left[...] = jnp.concatenate(
        [high, high, mid, mid, low, jnp.zeros_like(low), high, -FAR * side, -FAR * (1.0 - side)] + ones + norms, axis=0
    ).T.astype(jnp.bfloat16)
    sample[...] = jnp.zeros_like(sample)
    near = above.astype(jnp.int32) + below.astype(jnp.int32)
    pl.semaphore_wait(barrier, half + 1 + near)

    def part(c, l):
        return back.at[l, spot, parity, odd] if c else front.at[l, odd, parity, spot]

    def pair(c, l):
        return back.at[l, spot, parity] if c else front.at[l, odd, parity]

    def along(c, l, down):
        return remote(part(c, l), part(c, l), s_z.at[c, down, l], r_z.at[c, l], *there(line + 1 - 2 * down, odd, spot, parity))

    def to_mate(ref, send, recv):
        return remote(ref, ref, send, recv, *there(line, 1 - odd, spot, parity))

    def to_spot(ref, k, send, recv):
        return remote(ref, ref, send, recv, *there(line, odd, (spot + k) % half, parity))

    def hop(c, l):
        if c:
            return [to_mate(part(1, l), s_a.at[1, l, 0], r_a.at[1, l, 0])]
        return [to_spot(part(0, l), k, s_a.at[0, l, k], r_a.at[0, l, k]) for k in range(1, half)]

    def leap(c, l):
        if c:
            return [to_spot(pair(1, l), k, s_b.at[1, l, k], r_b.at[1, l, k]) for k in range(1, half)]
        return [to_mate(pair(0, l), s_b.at[0, l, 0], r_b.at[0, l, 0])]

    def cross(c, l, j):
        ref = back.at[l, j, parity] if c else front.at[l, j, parity]
        return remote(ref, ref, s_c.at[c, l, j], r_c.at[c, l, j], *there(line, odd, spot, 1 - parity))

    def go(copies):
        for copy in copies:
            copy.start()

    def come(copies):
        for copy in copies:
            copy.wait_recv()

    def leave(copies):
        for copy in copies:
            copy.wait_send()

    reach = jnp.minimum(line, lines - 1 - line)
    far = jnp.where(line < lines - 1 - line, 1, -1)

    def origin(n):
        return line + jnp.where(n <= 2 * reach, (2 * (n % 2) - 1) * ((n + 1) // 2), far * (n - reach))

    def upward(l):
        return (l <= line) & above

    def downward(l):
        return (l >= line) & below

    def arrive(n, own=False):
        l = origin(n)
        for c in range(2):
            if not own:
                along(c, l, 0).wait_recv()
            pl.when(upward(l))(along(c, l, 0).start)
            pl.when(downward(l))(along(c, l, 1).start)
            go(hop(c, l))

    def meet(n):
        l = origin(n)
        for c in range(2):
            come(hop(c, l))
            go(leap(c, l))
            cross(c, l, spot if c else odd).start()

    def add(l, p):
        terms = []
        for o in range(2):
            for s in range(half):
                pack = front[l, o, p, s]
                body, head, foot = pack[:split], pack[split : split + 16, :local], pack[split + 16 :, :local]
                right = jnp.concatenate([head, head, head, foot], axis=0)
                tile = jnp.exp(dot(left[...], right, ((1,), (0,)), None)).astype(jnp.bfloat16)
                test = jnp.concatenate([body, back[l, s, p, o]], axis=0)
                terms.append(dot(tile, test, ((1,), (0,)), None))
        while len(terms) > 1:
            terms = [a + b for a, b in zip(terms[::2], terms[1::2])] + terms[len(terms) // 2 * 2 :]
        sample[...] += terms[0]

    def close(n):
        l = origin(n)
        come(leap(0, l))
        cross(0, l, 1 - odd).start()
        for k, copy in enumerate(leap(1, l), 1):
            copy.wait_recv()
            cross(1, l, (spot + half - k) % half).start()
        add(l, parity)

    def last(n):
        l = origin(n)
        come([cross(0, l, j) for j in range(2)] + [cross(1, l, j) for j in range(half)])
        add(l, 1 - parity)

    arrive(0, True)
    meet(0)
    each(1, lines, arrive)

    def turn(n):
        meet(n)
        close(n - 1)
        last(n - 1)

    each(1, lines, turn)
    close(lines - 1)
    last(lines - 1)

    def settle(l):
        for c in range(2):
            pl.when(upward(l))(along(c, l, 0).wait_send)
            pl.when(downward(l))(along(c, l, 1).wait_send)
            leave(hop(c, l) + leap(c, l))
        leave([cross(0, l, j) for j in range(2)] + [cross(1, l, j) for j in range(half)])

    each(0, lines, settle)

    count = rows * half
    partner = col + 1 - 2 * parity
    total = sample[...]
    index = row * half + spot

    def place(i):
        return i // half, 2 * (i % half) + parity

    square[...] = dot(total.T, total, ((1,), (0,))).reshape(square.shape)
    trade = remote(square.at[1 - parity], mate, s_mate.at[0], r_mate.at[0], row, partner)
    trade.start()
    trade.wait()
    mine[...] = square[parity] + mate[...]

    def scatter(k):
        there = (index + k) % count
        r, c = place(there)
        return remote(mine.at[there], piece.at[k], s_piece.at[k], r_piece.at[k], r, c)

    each(1, count, lambda k: scatter(k).start())
    each(1, count, lambda k: scatter(k).wait())
    piece[0] = mine[index]
    done[...] = jnp.sum(piece[...], axis=0)
    gram[parity, index] = done[...]

    def collect(k):
        r, c = place((index + k) % count)
        return remote(done, gram.at[parity, index], s_done.at[k], r_done.at[k], r, c)

    def pass_on(k):
        there = (index + count - k) % count
        return remote(gram.at[parity, there], gram.at[parity, there], s_over.at[k], r_over.at[k], row, partner)

    def relay(k):
        collect(k).wait_recv()
        pass_on(k).start()

    own = remote(done, gram.at[parity, index], s_over.at[0], r_over.at[0], row, partner)
    each(1, count, lambda k: collect(k).start())
    own.start()
    each(1, count, relay)
    own.wait()
    each(1, count, lambda k: pass_on(k).wait())
    each(1, count, lambda k: collect(k).wait_send())


def sketch_gram(points, tests, rank, boundary, scales, rows, cols):
    local, ranks = tests.shape
    lines, half, count = rows // 2, cols // 2, rows * cols // 2
    lanes = 3 * (8 * ((points.shape[0] + 7) // 8)) + 8
    split = (local - lanes) // 32 * 16
    share = ranks // 2 // count
    f32 = jnp.float32
    dma = pltpu.SemaphoreType.DMA
    wide = max(2, half)
    sample, gram = pl.pallas_call(
        functools.partial(sample_kernel, rows, cols),
        out_shape=(
            jax.ShapeDtypeStruct((local, ranks), f32),
            jax.ShapeDtypeStruct((2, count, share, ranks), f32),
        ),
        in_specs=[VMEM, VMEM, VMEM, SMEM, SMEM],
        out_specs=(VMEM, VMEM),
        scratch_shapes=[
            pltpu.VMEM((lines, 2, 2, half, split + lanes, ranks), tests.dtype),
            pltpu.VMEM((lines, half, 2, 2, local - split, ranks), tests.dtype),
            pltpu.VMEM((local, 2 * lanes), tests.dtype),
            pltpu.VMEM((2, count, share, ranks), f32),
            pltpu.VMEM((count, share, ranks), f32),
            pltpu.VMEM((count, share, ranks), f32),
            pltpu.VMEM((count, share, ranks), f32),
            pltpu.VMEM((share, ranks), f32),
            dma((2, 2, lines)), dma((2, lines)),
            dma((2, lines, wide)), dma((2, lines, wide)),
            dma((2, lines, wide)), dma((2, lines, wide)),
            dma((2, lines, wide)), dma((2, lines, wide)),
            dma((1,)), dma((1,)), dma((count,)), dma((count,)), dma((count,)), dma((count,)), dma((count,)), dma((count,)),
        ],
        compiler_params=pltpu.CompilerParams(collective_id=0, has_side_effects=True),
        name="sketch_gram",
    )(points, tests, rank[None], boundary, scales)
    return sample, gram.reshape(ranks, ranks)


def factor_block(a):
    size, wide = a.shape[0], 8
    shape = (wide, size)
    lane = lax.broadcasted_iota(jnp.int32, shape, 1)
    line = lax.broadcasted_iota(jnp.int32, shape, 0)

    def spread(x):
        return jnp.broadcast_to(x, shape)

    blocks = [a[i : i + wide] for i in range(0, size, wide)]
    upper, inverse = [], []
    for b in range(size // wide):
        at = b * wide
        inside = (lane >= at) & (lane < at + wide)
        x = blocks[b]
        y = jnp.where(inside, jnp.where(lane - at == line, 1.0, 0.0), x)
        marks = [spread(x[:, at + u : at + u + 1]) for u in range(wide)]
        over, root = jnp.zeros(shape, jnp.float32), jnp.zeros(shape, jnp.float32)
        for s in range(wide):
            pivot = spread(marks[s][s : s + 1])
            inv = 1.0 / pivot
            over = jnp.where(line == s, inv, over)
            root = jnp.where(line == s, pivot, root)
            if s + 1 < wide:
                low = jnp.where(line > s, marks[s] * inv, 0.0)
                for u in range(s + 1, wide):
                    marks[u] = marks[u] - low * spread(marks[u][s : s + 1])
                x = x - low * spread(x[s : s + 1])
                y = y - low * spread(y[s : s + 1])
        z = y * over
        for s in range(wide - 1, 0, -1):
            z = z - jnp.where(line < s, marks[s] * over, 0.0) * spread(z[s : s + 1])
        rows = [spread(z[t : t + 1]) for t in range(wide)]
        for i in range(b + 1, size // wide):
            old = blocks[i]
            parts = [spread(old[:, at + t : at + t + 1]) * rows[t] for t in range(wide)]
            while len(parts) > 1:
                parts = [p + q for p, q in zip(parts[::2], parts[1::2])]
            blocks[i] = jnp.where(inside, 0.0, old) - parts[0]
        root = lax.rsqrt(root)
        upper.append(jnp.where(lane >= at + line, x * root, 0.0))
        inverse.append(jnp.where(lane <= at + line, y * root, 0.0))
    return jnp.concatenate(upper, axis=0), jnp.concatenate(inverse, axis=0)


def finish_kernel(scale, gram, sample, basis, factor, up, low):
    ranks = gram.shape[0]
    half = ranks // 2
    mean = gram[...] * scale
    same = lax.broadcasted_iota(jnp.int32, (ranks, ranks), 0) == lax.broadcasted_iota(jnp.int32, (ranks, ranks), 1)
    trace = jnp.sum(jnp.sum(jnp.where(same, mean, 0.0), axis=1, keepdims=True), axis=0, keepdims=True)
    factor[...] = jnp.where(same, mean + (0.1 / ranks) * trace, mean)
    cross = factor[:half, half:]

    def one(index):
        start = pl.multiple_of(index * half, half)
        block = factor[pl.ds(start, half), pl.ds(start, half)]
        u, m = factor_block(block)
        up[index] = u
        low[index] = m

        @pl.when(index == 0)
        def _():
            lift = dot(m, cross, ((1,), (0,)))
            up[2] = lift
            factor[half:, half:] = factor[half:, half:] - dot(lift.T, lift, ((1,), (0,)))

    each(0, 2, one)
    lift = up[2]
    first = dot(sample[:, :half], low[0], ((1,), (1,)))
    second = dot(sample[:, half:] - dot(first, lift, ((1,), (0,))), low[1], ((1,), (1,)))
    basis[:, :half] = first
    basis[:, half:] = second
    factor[:half, :half] = up[0].T
    factor[:half, half:] = jnp.zeros((half, half), jnp.float32)
    factor[half:, :half] = lift.T
    factor[half:, half:] = up[1].T


def finish(gram, sample, everyone):
    ranks = gram.shape[0]
    half = ranks // 2
    return pl.pallas_call(
        functools.partial(finish_kernel, 1.0 / everyone),
        out_shape=(
            jax.ShapeDtypeStruct(sample.shape, jnp.float32),
            jax.ShapeDtypeStruct(gram.shape, jnp.float32),
        ),
        in_specs=[VMEM, VMEM],
        out_specs=(VMEM, VMEM),
        scratch_shapes=[pltpu.VMEM((3, half, half), jnp.float32), pltpu.VMEM((2, half, half), jnp.float32)],
        name="finish",
    )(gram, sample)


def body(rows, cols, points, sketch, rank, boundary, scales):
    sample, gram = sketch_gram(points, sketch, rank, boundary, scales, rows, cols)
    return finish(gram, sample, rows * cols * points.shape[1])


def solution(mesh):
    placed = (P(None, ("row", "col")), P(("row", "col"), None), P(("row", "col")), P(), P())
    return jax.shard_map(
        functools.partial(body, mesh.shape["row"], mesh.shape["col"]),
        mesh=mesh,
        in_specs=placed,
        out_specs=(P(("row", "col"), None), P()),
        check_vma=False,
    )
```

time: 66.4 us -> 58 us (0.87)
  Pallas kernels: 64.9 us -> 56.5 us
    pallas_call x2 -> x1, Pallas kernels: 51.2 us -> 42.8 us  [sketch_gram(): pl.pallas_call(functools.partial(sample_kernel, rows, cols), out_shape=(j...]
where the time goes in v1:
time: 58 us; the launch traced here: 57.8 us
  Pallas kernels  56.5 us (97%)
  between operations  1.28 us (2%)
    pallas_call x1, Pallas kernels, sketch_gram(): pl.pallas_call(functools.partial(sample_kernel, rows, cols), out_shape=(j...  42.8 us
    pallas_call x1, Pallas kernels, finish(): pl.pallas_call(functools.partial(finish_kernel, 1.0 / everyone), out_shap...  13.8 us

profile of v1, /device:TPU:0, one launch (start us, length us, event | category | flops | bytes accessed | tf_op | source)
XLA Modules:
  0.0 57.8 jit_solution(16186398675396823414)
XLA Ops:
  1.3 42.8 %sketch_gram.1 = (f32[160,256]{1,0:T(8,128)}, f32[2,16,8,256]{3,2,1,0:T(8,128)}) custom-call(f32[8,160]{1,0:T(8,128)} %points.1, bf16[160,256]{1,0:T(8,128)(2,1)} %tests.1, s32[1,160]{1,0:T(1,128)} %bitcast.3, s32[1]{0:T(128)S(6)} %copy.7.boundary, f32[8]{0:T(128)} %scales.1), custom_call_target="tpu_custom_call" | custom-call | tf_op jit(solution)/shard_map/sketch_gram/pallas_call | solution.py:280
  44.0 13.8 %finish.1 = (f32[160,256]{1,0:T(8,128)}, f32[256,256]{1,0:T(8,128)}) custom-call(f32[256,256]{1,0:T(8,128)} %bitcast.2, f32[160,256]{1,0:T(8,128)} %get-tuple-element.5.sample), custom_call_target="tpu_custom_call" | custom-call | tf_op jit(solution)/shard_map/finish/pallas_call | solution.py:391

commit v2 on v1

--- a/solution.py
+++ b/solution.py
@@ -100,14 +100,10 @@
         [high, high, mid, mid, low, jnp.zeros_like(low), high, -FAR * side, -FAR * (1.0 - side)] + ones + norms, axis=0
     ).T.astype(jnp.bfloat16)
     sample[...] = jnp.zeros_like(sample)
-    near = above.astype(jnp.int32) + below.astype(jnp.int32)
-    pl.semaphore_wait(barrier, half + 1 + near)
+    pl.semaphore_wait(barrier, half + 1 + above.astype(jnp.int32) + below.astype(jnp.int32))
 
     def part(c, l):
         return back.at[l, spot, parity, odd] if c else front.at[l, odd, parity, spot]
-
-    def pair(c, l):
-        return back.at[l, spot, parity] if c else front.at[l, odd, parity]
 
     def along(c, l, down):
         return remote(part(c, l), part(c, l), s_z.at[c, down, l], r_z.at[c, l], *there(line + 1 - 2 * down, odd, spot, parity))
@@ -123,10 +119,16 @@
             return [to_mate(part(1, l), s_a.at[1, l, 0], r_a.at[1, l, 0])]
         return [to_spot(part(0, l), k, s_a.at[0, l, k], r_a.at[0, l, k]) for k in range(1, half)]
 
-    def leap(c, l):
+    def leap(c, l, k):
         if c:
-            return [to_spot(pair(1, l), k, s_b.at[1, l, k], r_b.at[1, l, k]) for k in range(1, half)]
-        return [to_mate(pair(0, l), s_b.at[0, l, 0], r_b.at[0, l, 0])]
+            return [
+                to_spot(back.at[l, spot, parity, (odd + k) % 2], j, s_b.at[1, l, k, j], r_b.at[1, l, k, j])
+                for j in range(1, half)
+            ]
+        return [to_mate(front.at[l, odd, parity, (spot + half - k) % half], s_b.at[0, l, k, 0], r_b.at[0, l, k, 0])]
+
+    def leaps(c, l):
+        return [copy for k in range(2 if c else half) for copy in leap(c, l, k)]
 
     def cross(c, l, j):
         ref = back.at[l, j, parity] if c else front.at[l, j, parity]
@@ -163,13 +165,14 @@
                 along(c, l, 0).wait_recv()
             pl.when(upward(l))(along(c, l, 0).start)
             pl.when(downward(l))(along(c, l, 1).start)
-            go(hop(c, l))
+            go(hop(c, l) + leap(c, l, 0))
 
     def meet(n):
         l = origin(n)
         for c in range(2):
-            come(hop(c, l))
-            go(leap(c, l))
+            for k, copy in enumerate(hop(c, l), 1):
+                copy.wait_recv()
+                go(leap(c, l, k))
             cross(c, l, spot if c else odd).start()
 
     def add(l, p):
@@ -188,36 +191,42 @@
 
     def close(n):
         l = origin(n)
-        come(leap(0, l))
+        come(leaps(0, l))
         cross(0, l, 1 - odd).start()
-        for k, copy in enumerate(leap(1, l), 1):
-            copy.wait_recv()
-            cross(1, l, (spot + half - k) % half).start()
-        add(l, parity)
+        come(leaps(1, l))
+        for k in range(1, half):
+            cross(1, l, (spot + k) % half).start()
+
+    def near(n):
+        add(origin(n), parity)
 
     def last(n):
         l = origin(n)
         come([cross(0, l, j) for j in range(2)] + [cross(1, l, j) for j in range(half)])
         add(l, 1 - parity)
 
+    def advance(n):
+        arrive(n + 1)
+        meet(n)
+
     arrive(0, True)
-    meet(0)
-    each(1, lines, arrive)
-
-    def turn(n):
-        meet(n)
-        close(n - 1)
+    each(0, lines - 1, advance)
+    meet(lines - 1)
+    close(0)
+
+    def finish_line(n):
+        close(n)
+        near(n - 1)
         last(n - 1)
 
-    each(1, lines, turn)
-    close(lines - 1)
+    each(1, lines, finish_line)
+    near(lines - 1)
     last(lines - 1)
-
     def settle(l):
         for c in range(2):
             pl.when(upward(l))(along(c, l, 0).wait_send)
             pl.when(downward(l))(along(c, l, 1).wait_send)
-            leave(hop(c, l) + leap(c, l))
+            leave(hop(c, l) + leaps(c, l))
         leave([cross(0, l, j) for j in range(2)] + [cross(1, l, j) for j in range(half)])
 
     each(0, lines, settle)
@@ -296,7 +305,7 @@
             pltpu.VMEM((share, ranks), f32),
             dma((2, 2, lines)), dma((2, lines)),
             dma((2, lines, wide)), dma((2, lines, wide)),
-            dma((2, lines, wide)), dma((2, lines, wide)),
+            dma((2, lines, wide, wide)), dma((2, lines, wide, wide)),
             dma((2, lines, wide)), dma((2, lines, wide)),
             dma((1,)), dma((1,)), dma((count,)), dma((count,)), dma((count,)), dma((count,)), dma((count,)), dma((count,)),
         ],
@@ -306,8 +315,20 @@
     return sample, gram.reshape(ranks, ranks)
 
 
-def factor_block(a):
-    size, wide = a.shape[0], 8
+def tree(parts):
+    while len(parts) > 1:
+        parts = [p + q for p, q in zip(parts[::2], parts[1::2])] + parts[len(parts) // 2 * 2 :]
+    return parts[0]
+
+
+def sixfold(a, b):
+    ah, am, al = thirds(a)
+    bh, bm, bl = thirds(b)
+    return jnp.concatenate([ah, ah, am, ah, al, am], axis=0), jnp.concatenate([bh, bm, bh, bl, bh, bm], axis=0)
+
+
+def factor_block(a, zero):
+    size, wide, width = a.shape[0], 8, 32
     shape = (wide, size)
     lane = lax.broadcasted_iota(jnp.int32, shape, 1)
     line = lax.broadcasted_iota(jnp.int32, shape, 0)
@@ -315,39 +336,61 @@
     def spread(x):
         return jnp.broadcast_to(x, shape)
 
-    blocks = [a[i : i + wide] for i in range(0, size, wide)]
+    def column(x, at):
+        return jnp.take_along_axis(x, zero + at, axis=1)
+
+    rest = a
     upper, inverse = [], []
-    for b in range(size // wide):
-        at = b * wide
-        inside = (lane >= at) & (lane < at + wide)
-        x = blocks[b]
-        y = jnp.where(inside, jnp.where(lane - at == line, 1.0, 0.0), x)
-        marks = [spread(x[:, at + u : at + u + 1]) for u in range(wide)]
-        over, root = jnp.zeros(shape, jnp.float32), jnp.zeros(shape, jnp.float32)
-        for s in range(wide):
-            pivot = spread(marks[s][s : s + 1])
-            inv = 1.0 / pivot
-            over = jnp.where(line == s, inv, over)
-            root = jnp.where(line == s, pivot, root)
-            if s + 1 < wide:
-                low = jnp.where(line > s, marks[s] * inv, 0.0)
+    for begin in range(0, size, width):
+        end = begin + width
+        blocks = [rest[i : i + wide] for i in range(0, width, wide)]
+        us, ms = [], []
+        marks = [column(blocks[0], begin + u) for u in range(wide)]
+        for at in range(begin, end, wide):
+            inside = (lane >= at) & (lane < at + wide)
+            x = blocks.pop(0)
+            z = jnp.where(inside, jnp.where(lane - at == line, 1.0, 0.0), x)
+            y = z
+            old = [[column(block, at + t) for t in range(wide)] for block in blocks]
+            ahead = [column(x, at + wide + u) for u in range(wide)] if blocks else []
+            fresh = [column(blocks[0], at + wide + u) for u in range(wide)] if blocks else []
+            over, root = jnp.zeros(shape, jnp.float32), jnp.zeros(shape, jnp.float32)
+            for s in range(wide):
+                pivot = spread(marks[s][s : s + 1])
+                inv = 1.0 / pivot
+                over = jnp.where(line == s, inv, over)
+                root = jnp.where(line == s, pivot, root)
+                ratio = marks[s] * inv
+                low = jnp.where(line > s, ratio, 0.0)
+                both = jnp.where(line == s, 0.0, ratio)
                 for u in range(s + 1, wide):
-                    marks[u] = marks[u] - low * spread(marks[u][s : s + 1])
-                x = x - low * spread(x[s : s + 1])
-                y = y - low * spread(y[s : s + 1])
-        z = y * over
-        for s in range(wide - 1, 0, -1):
-            z = z - jnp.where(line < s, marks[s] * over, 0.0) * spread(z[s : s + 1])
-        rows = [spread(z[t : t + 1]) for t in range(wide)]
-        for i in range(b + 1, size // wide):
-            old = blocks[i]
-            parts = [spread(old[:, at + t : at + t + 1]) * rows[t] for t in range(wide)]
-            while len(parts) > 1:
-                parts = [p + q for p, q in zip(parts[::2], parts[1::2])]
-            blocks[i] = jnp.where(inside, 0.0, old) - parts[0]
-        root = lax.rsqrt(root)
-        upper.append(jnp.where(lane >= at + line, x * root, 0.0))
-        inverse.append(jnp.where(lane <= at + line, y * root, 0.0))
+                    marks[u] = marks[u] - both * spread(marks[u][s : s + 1])
+                ahead = [c - both * spread(c[s : s + 1]) for c in ahead]
+                if s + 1 < wide:
+                    x = x - low * spread(x[s : s + 1])
+                    y = y - low * spread(y[s : s + 1])
+                z = z - both * spread(z[s : s + 1])
+            ahead = [c * over for c in ahead]
+            marks = [
+                f - tree([old[0][t] * spread(c[t : t + 1]) for t in range(wide)]) for f, c in zip(fresh, ahead)
+            ]
+            z = z * over
+            rows = [spread(z[t : t + 1]) for t in range(wide)]
+            blocks = [
+                jnp.where(inside, 0.0, block) - tree([c * r for c, r in zip(columns, rows)])
+                for block, columns in zip(blocks, old)
+            ]
+            root = lax.rsqrt(root)
+            us.append(jnp.where(lane >= at + line, x * root, 0.0))
+            ms.append(jnp.where(lane <= at + line, y * root, 0.0))
+        u, m = jnp.concatenate(us, axis=0), jnp.concatenate(ms, axis=0)
+        upper.append(u)
+        inverse.append(m)
+        if end < size:
+            left, right = sixfold(u, jnp.where(lax.broadcasted_iota(jnp.int32, u.shape, 1) >= end, u, m))
+            change = dot(left.T[end:].astype(jnp.bfloat16), right.astype(jnp.bfloat16), ((1,), (0,)), None)
+            spot = lax.broadcasted_iota(jnp.int32, change.shape, 1)
+            rest = jnp.where((spot >= begin) & (spot < end), 0.0, rest[width:]) - change
     return jnp.concatenate(upper, axis=0), jnp.concatenate(inverse, axis=0)
 
 
@@ -359,11 +402,12 @@
     trace = jnp.sum(jnp.sum(jnp.where(same, mean, 0.0), axis=1, keepdims=True), axis=0, keepdims=True)
     factor[...] = jnp.where(same, mean + (0.1 / ranks) * trace, mean)
     cross = factor[:half, half:]
+    zero = (factor[:8, :half] * 0.0).astype(jnp.int32)
 
     def one(index):
         start = pl.multiple_of(index * half, half)
         block = factor[pl.ds(start, half), pl.ds(start, half)]
-        u, m = factor_block(block)
+        u, m = factor_block(block, zero)
         up[index] = u
         low[index] = m
 

time: 58 us -> 52 us (0.90)
  Pallas kernels: 56.5 us -> 50.5 us
    pallas_call x1, Pallas kernels: 13.8 us -> 9.19 us  [finish(): pl.pallas_call(functools.partial(finish_kernel, 1.0 / everyone), out_shap...]
    pallas_call x1, Pallas kernels: 42.8 us -> 41.3 us  [sketch_gram(): pl.pallas_call(functools.partial(sample_kernel, rows, cols), out_shape=(j...]
where the time goes in v2:
time: 52 us; the launch traced here: 51.8 us
  Pallas kernels  50.5 us (97%)
  between operations  1.28 us (2%)
    pallas_call x1, Pallas kernels, sketch_gram(): pl.pallas_call(functools.partial(sample_kernel, rows, cols), out_shape=(j...  41.3 us
    pallas_call x1, Pallas kernels, finish(): pl.pallas_call(functools.partial(finish_kernel, 1.0 / everyone), out_shap...  9.19 us

profile of v2, /device:TPU:0, one launch (start us, length us, event | category | flops | bytes accessed | tf_op | source)
XLA Modules:
  0.0 51.8 jit_solution(2961548153418584184)
XLA Ops:
  1.3 41.3 %sketch_gram.1 = (f32[160,256]{1,0:T(8,128)}, f32[2,16,8,256]{3,2,1,0:T(8,128)}) custom-call(f32[8,160]{1,0:T(8,128)} %points.1, bf16[160,256]{1,0:T(8,128)(2,1)} %tests.1, s32[1,160]{1,0:T(1,128)} %bitcast.3, s32[1]{0:T(128)S(6)} %copy.7.boundary, f32[8]{0:T(128)} %scales.1), custom_call_target="tpu_custom_call" | custom-call | tf_op jit(solution)/shard_map/sketch_gram/pallas_call | solution.py:289
  42.6 9.2 %finish.1 = (f32[160,256]{1,0:T(8,128)}, f32[256,256]{1,0:T(8,128)}) custom-call(f32[256,256]{1,0:T(8,128)} %bitcast.2, f32[160,256]{1,0:T(8,128)} %get-tuple-element.5.sample), custom_call_target="tpu_custom_call" | custom-call | tf_op jit(solution)/shard_map/finish/pallas_call | solution.py:435

commit v3 on v2

--- a/solution.py
+++ b/solution.py
@@ -11,6 +11,7 @@
 FAR = 4992.0
 VMEM = pl.BlockSpec(memory_space=pltpu.VMEM)
 SMEM = pl.BlockSpec(memory_space=pltpu.SMEM)
+HBM = pl.BlockSpec(memory_space=pltpu.HBM)
 
 
 def dot(a, b, dims, precision=HIGHEST):
@@ -45,8 +46,8 @@
 
 
 def sample_kernel(
-    rows, cols, points, tests, rank, boundary, scales, sample, gram, front, back, left,
-    square, mate, mine, piece, done,
+    rows, cols, points_hbm, tests, rank_hbm, boundary, scales_hbm, sample, gram, front, back, left,
+    points, rank, scales, s_in, square, mate, mine, piece, done,
     s_z, r_z, s_a, r_a, s_b, r_b, s_c, r_c,
     s_mate, r_mate, s_piece, r_piece, s_done, r_done, s_over, r_over,
 ):
@@ -81,6 +82,20 @@
     greet(line, 1 - odd, spot, parity)
     greet(line, odd, spot, 1 - parity)
 
+    loads = [
+        pltpu.make_async_copy(src, dst, s_in.at[i])
+        for i, (src, dst) in enumerate([
+            (scales_hbm, scales),
+            (points_hbm, points),
+            (rank_hbm, rank),
+            (tests.at[:split], front.at[line, odd, parity, spot, :split]),
+            (tests.at[split:], back.at[line, spot, parity, odd]),
+        ])
+    ]
+    for load in loads:
+        load.start()
+    for load in loads[:3]:
+        load.wait()
     index = lax.broadcasted_iota(jnp.int32, points.shape, 0)
     scale = jnp.ones(points.shape, jnp.float32)
     for i in range(dims):
@@ -93,13 +108,13 @@
     ones = [jnp.ones_like(side)] * 3
     info = jnp.concatenate([high, mid, low, side, 1.0 - side] + norms + ones, axis=0)
     wide = jnp.zeros((info.shape[0], tests.shape[1] - local), jnp.float32)
-    front[line, odd, parity, spot, :split] = tests[:split]
     front[line, odd, parity, spot, split:] = jnp.concatenate([info, wide], axis=1).astype(jnp.bfloat16)
-    back[line, spot, parity, odd] = tests[split:]
     left[...] = jnp.concatenate(
         [high, high, mid, mid, low, jnp.zeros_like(low), high, -FAR * side, -FAR * (1.0 - side)] + ones + norms, axis=0
     ).T.astype(jnp.bfloat16)
     sample[...] = jnp.zeros_like(sample)
+    for load in loads[3:]:
+        load.wait()
     pl.semaphore_wait(barrier, half + 1 + above.astype(jnp.int32) + below.astype(jnp.int32))
 
     def part(c, l):
@@ -275,6 +290,10 @@
     own.wait()
     each(1, count, lambda k: pass_on(k).wait())
     each(1, count, lambda k: collect(k).wait_send())
+
+
+def far(x):
+    return pltpu.with_memory_space_constraint(x, pltpu.HBM)
 
 
 def sketch_gram(points, tests, rank, boundary, scales, rows, cols):
@@ -292,12 +311,13 @@
             jax.ShapeDtypeStruct((local, ranks), f32),
             jax.ShapeDtypeStruct((2, count, share, ranks), f32),
         ),
-        in_specs=[VMEM, VMEM, VMEM, SMEM, SMEM],
+        in_specs=[HBM, HBM, HBM, SMEM, HBM],
         out_specs=(VMEM, VMEM),
         scratch_shapes=[
             pltpu.VMEM((lines, 2, 2, half, split + lanes, ranks), tests.dtype),
             pltpu.VMEM((lines, half, 2, 2, local - split, ranks), tests.dtype),
             pltpu.VMEM((local, 2 * lanes), tests.dtype),
+            pltpu.VMEM(points.shape, f32), pltpu.VMEM((1, local), rank.dtype), pltpu.SMEM(scales.shape, f32), dma((5,)),
             pltpu.VMEM((2, count, share, ranks), f32),
             pltpu.VMEM((count, share, ranks), f32),
             pltpu.VMEM((count, share, ranks), f32),
@@ -309,9 +329,13 @@
             dma((2, lines, wide)), dma((2, lines, wide)),
             dma((1,)), dma((1,)), dma((count,)), dma((count,)), dma((count,)), dma((count,)), dma((count,)), dma((count,)),
         ],
-        compiler_params=pltpu.CompilerParams(collective_id=0, has_side_effects=True),
+        compiler_params=pltpu.CompilerParams(
+            collective_id=0,
+            has_side_effects=True,
+            vmem_limit_bytes=2 * rows * cols * (local + lanes) * ranks + 8 * 2**20,
+        ),
         name="sketch_gram",
-    )(points, tests, rank[None], boundary, scales)
+    )(far(points), far(tests), far(rank[None]), boundary, far(scales))
     return sample, gram.reshape(ranks, ranks)
 
 
@@ -337,7 +361,7 @@
         return jnp.broadcast_to(x, shape)
 
     def column(x, at):
-        return jnp.take_along_axis(x, zero + at, axis=1)
+        return jnp.take_along_axis(x, zero + at, axis=1, mode="promise_in_bounds")
 
     rest = a
     upper, inverse = [], []
@@ -394,44 +418,35 @@
     return jnp.concatenate(upper, axis=0), jnp.concatenate(inverse, axis=0)
 
 
-def finish_kernel(scale, gram, sample, basis, factor, up, low):
+def product(a, b, dims):
+    (i,), (j,) = dims
+    ah, am, al = [part.astype(jnp.bfloat16) for part in thirds(a)]
+    bh, bm, bl = [part.astype(jnp.bfloat16) for part in thirds(b)]
+    return dot(jnp.concatenate([ah, ah, am, ah, al, am], axis=i), jnp.concatenate([bh, bm, bh, bl, bh, bm], axis=j), dims, None)
+
+
+def finish_kernel(scale, gram, sample, basis, factor):
     ranks = gram.shape[0]
     half = ranks // 2
     mean = gram[...] * scale
     same = lax.broadcasted_iota(jnp.int32, (ranks, ranks), 0) == lax.broadcasted_iota(jnp.int32, (ranks, ranks), 1)
-    trace = jnp.sum(jnp.sum(jnp.where(same, mean, 0.0), axis=1, keepdims=True), axis=0, keepdims=True)
-    factor[...] = jnp.where(same, mean + (0.1 / ranks) * trace, mean)
-    cross = factor[:half, half:]
-    zero = (factor[:8, :half] * 0.0).astype(jnp.int32)
-
-    def one(index):
-        start = pl.multiple_of(index * half, half)
-        block = factor[pl.ds(start, half), pl.ds(start, half)]
-        u, m = factor_block(block, zero)
-        up[index] = u
-        low[index] = m
-
-        @pl.when(index == 0)
-        def _():
-            lift = dot(m, cross, ((1,), (0,)))
-            up[2] = lift
-            factor[half:, half:] = factor[half:, half:] - dot(lift.T, lift, ((1,), (0,)))
-
-    each(0, 2, one)
-    lift = up[2]
-    first = dot(sample[:, :half], low[0], ((1,), (1,)))
-    second = dot(sample[:, half:] - dot(first, lift, ((1,), (0,))), low[1], ((1,), (1,)))
+    trace = jnp.sum(jnp.sum(jnp.where(same, mean, 0.0), axis=0, keepdims=True), axis=1, keepdims=True)
+    shifted = jnp.where(same, mean + (0.1 / ranks) * trace, mean)
+    zero = (mean[:8, :half] * 0.0).astype(jnp.int32)
+    up, low = factor_block(shifted[:half, :half], zero)
+    lift = product(low, shifted[:half, half:], ((1,), (0,)))
+    up2, low2 = factor_block(shifted[half:, half:] - product(lift.T, lift, ((1,), (0,))), zero)
+    first = product(sample[:, :half], low, ((1,), (1,)))
+    rest = sample[:, half:] - product(first, lift, ((1,), (0,)))
     basis[:, :half] = first
-    basis[:, half:] = second
-    factor[:half, :half] = up[0].T
+    basis[:, half:] = product(rest, low2, ((1,), (1,)))
+    factor[:half, :half] = up.T
     factor[:half, half:] = jnp.zeros((half, half), jnp.float32)
     factor[half:, :half] = lift.T
-    factor[half:, half:] = up[1].T
+    factor[half:, half:] = up2.T
 
 
 def finish(gram, sample, everyone):
-    ranks = gram.shape[0]
-    half = ranks // 2
     return pl.pallas_call(
         functools.partial(finish_kernel, 1.0 / everyone),
         out_shape=(
@@ -440,7 +455,7 @@
         ),
         in_specs=[VMEM, VMEM],
         out_specs=(VMEM, VMEM),
-        scratch_shapes=[pltpu.VMEM((3, half, half), jnp.float32), pltpu.VMEM((2, half, half), jnp.float32)],
+        compiler_params=pltpu.CompilerParams(vmem_limit_bytes=8 * 2**20),
         name="finish",
     )(gram, sample)
 

time: 52 us -> 48.7 us (0.937)
  Pallas kernels: 50.5 us -> 47.2 us
    pallas_call x1, Pallas kernels: 9.19 us -> 7.48 us  [finish(): pl.pallas_call(functools.partial(finish_kernel, 1.0 / everyone), out_shap...]
    pallas_call x1, Pallas kernels: 41.3 us -> 39.7 us  [sketch_gram(): pl.pallas_call(functools.partial(sample_kernel, rows, cols), out_shape=(j...]
where the time goes in v3:
time: 48.7 us; the launch traced here: 48.5 us
  Pallas kernels  47.2 us (97%)
  between operations  1.28 us (3%)
    pallas_call x1, Pallas kernels, sketch_gram(): pl.pallas_call(functools.partial(sample_kernel, rows, cols), out_shape=(j...  39.7 us
    pallas_call x1, Pallas kernels, finish(): pl.pallas_call(functools.partial(finish_kernel, 1.0 / everyone), out_shap...  7.48 us

profile of v3, /device:TPU:0, one launch (start us, length us, event | category | flops | bytes accessed | tf_op | source)
XLA Modules:
  0.0 48.5 jit_solution(6884472709373349306)
XLA Ops:
  1.3 39.7 %sketch_gram.1 = (f32[160,256]{1,0:T(8,128)S(1)}, f32[2,16,8,256]{3,2,1,0:T(8,128)S(1)}) custom-call(f32[8,160]{1,0:T(8,128)} %points_hbm.1, bf16[160,256]{1,0:T(8,128)(2,1)} %tests.1, s32[1,160]{1,0:T(1,128)} %bitcast.3, s32[1]{0:T(128)S(6)} %copy.7.boundary, f32[8]{0:T(128)} %scales_hbm.1), custom_call_target="tpu_custom_call" | custom-call | tf_op jit(solution)/shard_map/sketch_gram/pallas_call | solution.py:308
  41.0 7.5 %finish.1 = (f32[160,256]{1,0:T(8,128)}, f32[256,256]{1,0:T(8,128)}) custom-call(f32[256,256]{1,0:T(8,128)S(1)} %bitcast.2, f32[160,256]{1,0:T(8,128)S(1)} %get-tuple-element.5.sample), custom_call_target="tpu_custom_call" | custom-call | tf_op jit(solution)/shard_map/finish/pallas_call | solution.py:450

commit v4 on v3

--- a/solution.py
+++ b/solution.py
@@ -252,44 +252,89 @@
     index = row * half + spot
 
     def place(i):
-        return i // half, 2 * (i % half) + parity
-
-    square[...] = dot(total.T, total, ((1,), (0,))).reshape(square.shape)
-    trade = remote(square.at[1 - parity], mate, s_mate.at[0], r_mate.at[0], row, partner)
-    trade.start()
-    trade.wait()
+        return lax.div(i, half), 2 * lax.rem(i, half) + parity
+
+    ranks = total.shape[1]
+
+    def cut(ref, low):
+        return ref.at[:, ranks // 2 :] if low else ref
+
+    def cuts(ref, low):
+        return ref.at[:, :, ranks // 2 :] if low else ref
+
+    def mine_or(make, act):
+        for low in range(2):
+            pl.when(parity == low)(lambda low=low: act(make(low)))
+
+    def other(make, act):
+        for low in range(2):
+            pl.when(parity == 1 - low)(lambda low=low: act(make(low)))
+
+    def begin(copy):
+        copy.start()
+
+    def got(copy):
+        copy.wait_recv()
+
+    def sent(copy):
+        copy.wait_send()
+
+    def both(copy):
+        copy.wait()
+
+    square[...] = product(total, total, ((0,), (0,))).reshape(square.shape)
+
+    def trade(low):
+        return remote(cuts(square.at[low], low), cuts(mate, low), s_mate.at[0], r_mate.at[0], row, partner)
+
+    other(trade, begin)
+    mine_or(trade, got)
     mine[...] = square[parity] + mate[...]
 
     def scatter(k):
-        there = (index + k) % count
+        there = lax.rem(index + k, count)
         r, c = place(there)
-        return remote(mine.at[there], piece.at[k], s_piece.at[k], r_piece.at[k], r, c)
-
-    each(1, count, lambda k: scatter(k).start())
-    each(1, count, lambda k: scatter(k).wait())
+        return lambda low: remote(cut(mine.at[there], low), cut(piece.at[k], low), s_piece.at[k], r_piece.at[k], r, c)
+
+    each(1, count, lambda k: mine_or(scatter(k), begin))
+    each(1, count, lambda k: mine_or(scatter(k), both))
     piece[0] = mine[index]
     done[...] = jnp.sum(piece[...], axis=0)
     gram[parity, index] = done[...]
 
     def collect(k):
-        r, c = place((index + k) % count)
-        return remote(done, gram.at[parity, index], s_done.at[k], r_done.at[k], r, c)
+        r, c = place(lax.rem(index + k, count))
+        return lambda low: remote(cut(done, low), cut(gram.at[parity, index], low), s_done.at[k], r_done.at[k], r, c)
 
     def pass_on(k):
-        there = (index + count - k) % count
-        return remote(gram.at[parity, there], gram.at[parity, there], s_over.at[k], r_over.at[k], row, partner)
+        there = lax.rem(index + count - k, count)
+
+        def make(low):
+            ref = cut(gram.at[low, there], low)
+            return remote(ref, ref, s_over.at[k], r_over.at[k], row, partner)
+
+        return make
 
     def relay(k):
-        collect(k).wait_recv()
-        pass_on(k).start()
-
-    own = remote(done, gram.at[parity, index], s_over.at[0], r_over.at[0], row, partner)
-    each(1, count, lambda k: collect(k).start())
-    own.start()
+        mine_or(collect(k), got)
+        mine_or(pass_on(k), begin)
+
+    def own(low):
+        return remote(cut(done, low), cut(gram.at[low, index], low), s_over.at[0], r_over.at[0], row, partner)
+
+    each(1, count, lambda k: mine_or(collect(k), begin))
+    mine_or(own, begin)
     each(1, count, relay)
-    own.wait()
-    each(1, count, lambda k: pass_on(k).wait())
-    each(1, count, lambda k: collect(k).wait_send())
+    mine_or(own, sent)
+    other(own, got)
+
+    def last_waits(k):
+        mine_or(pass_on(k), sent)
+        other(pass_on(k), got)
+        mine_or(collect(k), sent)
+
+    each(1, count, last_waits)
+    other(trade, sent)
 
 
 def far(x):
@@ -426,16 +471,15 @@
 
 
 def finish_kernel(scale, gram, sample, basis, factor):
-    ranks = gram.shape[0]
-    half = ranks // 2
-    mean = gram[...] * scale
-    same = lax.broadcasted_iota(jnp.int32, (ranks, ranks), 0) == lax.broadcasted_iota(jnp.int32, (ranks, ranks), 1)
-    trace = jnp.sum(jnp.sum(jnp.where(same, mean, 0.0), axis=0, keepdims=True), axis=1, keepdims=True)
-    shifted = jnp.where(same, mean + (0.1 / ranks) * trace, mean)
-    zero = (mean[:8, :half] * 0.0).astype(jnp.int32)
-    up, low = factor_block(shifted[:half, :half], zero)
-    lift = product(low, shifted[:half, half:], ((1,), (0,)))
-    up2, low2 = factor_block(shifted[half:, half:] - product(lift.T, lift, ((1,), (0,))), zero)
+    half = gram.shape[0] // 2
+    head, cross, foot = [part * scale for part in (gram[:half, :half], gram[:half, half:], gram[half:, half:])]
+    same = lax.broadcasted_iota(jnp.int32, (half, half), 0) == lax.broadcasted_iota(jnp.int32, (half, half), 1)
+    trace = jnp.sum(jnp.sum(jnp.where(same, head + foot, 0.0), axis=0, keepdims=True), axis=1, keepdims=True)
+    shift = jnp.where(same, (0.05 / half) * trace, 0.0)
+    zero = (head[:8] * 0.0).astype(jnp.int32)
+    up, low = factor_block(head + shift, zero)
+    lift = product(low, cross, ((1,), (0,)))
+    up2, low2 = factor_block(foot + shift - product(lift.T, lift, ((1,), (0,))), zero)
     first = product(sample[:, :half], low, ((1,), (1,)))
     rest = sample[:, half:] - product(first, lift, ((1,), (0,)))
     basis[:, :half] = first

time: 48.7 us -> 47.8 us (0.982)
  Pallas kernels: 47.2 us -> 46.3 us
    pallas_call x1, Pallas kernels: 39.7 us -> 38.8 us  [sketch_gram(): pl.pallas_call(functools.partial(sample_kernel, rows, cols), out_shape=(j...]
where the time goes in v4:
time: 47.8 us; the launch traced here: 47.6 us
  Pallas kernels  46.3 us (97%)
  between operations  1.28 us (3%)
    pallas_call x1, Pallas kernels, sketch_gram(): pl.pallas_call(functools.partial(sample_kernel, rows, cols), out_shape=(j...  38.8 us
    pallas_call x1, Pallas kernels, finish(): pl.pallas_call(functools.partial(finish_kernel, 1.0 / everyone), out_shap...  7.46 us

profile of v4, /device:TPU:0, one launch (start us, length us, event | category | flops | bytes accessed | tf_op | source)
XLA Modules:
  0.0 47.6 jit_solution(1048077349007313599)
XLA Ops:
  1.3 38.8 %sketch_gram.1 = (f32[160,256]{1,0:T(8,128)S(1)}, f32[2,16,8,256]{3,2,1,0:T(8,128)S(1)}) custom-call(f32[8,160]{1,0:T(8,128)} %points_hbm.1, bf16[160,256]{1,0:T(8,128)(2,1)} %tests.1, s32[1,160]{1,0:T(1,128)} %bitcast.3, s32[1]{0:T(128)S(6)} %copy.7.boundary, f32[8]{0:T(128)} %scales_hbm.1), custom_call_target="tpu_custom_call" | custom-call | tf_op jit(solution)/shard_map/sketch_gram/pallas_call | solution.py:353
  40.1 7.5 %finish.1 = (f32[160,256]{1,0:T(8,128)}, f32[256,256]{1,0:T(8,128)}) custom-call(f32[256,256]{1,0:T(8,128)S(1)} %bitcast.2, f32[160,256]{1,0:T(8,128)S(1)} %get-tuple-element.5.sample), custom_call_target="tpu_custom_call" | custom-call | tf_op jit(solution)/shard_map/finish/pallas_call | solution.py:494

commit v5 on v4

--- a/solution.py
+++ b/solution.py
@@ -48,8 +48,7 @@
 def sample_kernel(
     rows, cols, points_hbm, tests, rank_hbm, boundary, scales_hbm, sample, gram, front, back, left,
     points, rank, scales, s_in, square, mate, mine, piece, done,
-    s_z, r_z, s_a, r_a, s_b, r_b, s_c, r_c,
-    s_mate, r_mate, s_piece, r_piece, s_done, r_done, s_over, r_over,
+    s_all, r_z, r_a, r_b, r_c, s_mate, r_mate, r_piece, r_done, r_over,
 ):
     row, col = lax.axis_index("row"), lax.axis_index("col")
     lines, half = rows // 2, cols // 2
@@ -117,11 +116,19 @@
         load.wait()
     pl.semaphore_wait(barrier, half + 1 + above.astype(jnp.int32) + below.astype(jnp.int32))
 
+    most = half - 1
+    hops, jumps = lines + 1 + lines * most, lines * max(half, 2 * most)
+
+    def send(kind, c, i):
+        begin = 0 if kind < 2 else hops + (jumps if kind > 2 else 0)
+        step = hops + jumps + lines * max(2, half)
+        return s_all.at[c * step + begin + i + (lines + 1 if kind == 1 else 0)]
+
     def part(c, l):
         return back.at[l, spot, parity, odd] if c else front.at[l, odd, parity, spot]
 
     def along(c, l, down):
-        return remote(part(c, l), part(c, l), s_z.at[c, down, l], r_z.at[c, l], *there(line + 1 - 2 * down, odd, spot, parity))
+        return remote(part(c, l), part(c, l), send(0, c, jnp.where((l == line) & (down == 1), lines, l)), r_z.at[c, l], *there(line + 1 - 2 * down, odd, spot, parity))
 
     def to_mate(ref, send, recv):
         return remote(ref, ref, send, recv, *there(line, 1 - odd, spot, parity))
@@ -131,23 +138,23 @@
 
     def hop(c, l):
         if c:
-            return [to_mate(part(1, l), s_a.at[1, l, 0], r_a.at[1, l, 0])]
-        return [to_spot(part(0, l), k, s_a.at[0, l, k], r_a.at[0, l, k]) for k in range(1, half)]
+            return [to_mate(part(1, l), send(1, 1, l), r_a.at[1, l, 0])]
+        return [to_spot(part(0, l), k, send(1, 0, l * most + k - 1), r_a.at[0, l, k - 1]) for k in range(1, half)]
 
     def leap(c, l, k):
         if c:
             return [
-                to_spot(back.at[l, spot, parity, (odd + k) % 2], j, s_b.at[1, l, k, j], r_b.at[1, l, k, j])
+                to_spot(back.at[l, spot, parity, (odd + k) % 2], j, send(2, 1, l * 2 * most + k * most + j - 1), r_b.at[1, l, k * most + j - 1])
                 for j in range(1, half)
             ]
-        return [to_mate(front.at[l, odd, parity, (spot + half - k) % half], s_b.at[0, l, k, 0], r_b.at[0, l, k, 0])]
+        return [to_mate(front.at[l, odd, parity, (spot + half - k) % half], send(2, 0, l * half + k), r_b.at[0, l, k])]
 
     def leaps(c, l):
         return [copy for k in range(2 if c else half) for copy in leap(c, l, k)]
 
     def cross(c, l, j):
         ref = back.at[l, j, parity] if c else front.at[l, j, parity]
-        return remote(ref, ref, s_c.at[c, l, j], r_c.at[c, l, j], *there(line, odd, spot, 1 - parity))
+        return remote(ref, ref, send(3, c, l * (half if c else 2) + j), r_c.at[c, l, j], *there(line, odd, spot, 1 - parity))
 
     def go(copies):
         for copy in copies:
@@ -244,7 +251,6 @@
             leave(hop(c, l) + leaps(c, l))
         leave([cross(0, l, j) for j in range(2)] + [cross(1, l, j) for j in range(half)])
 
-    each(0, lines, settle)
 
     count = rows * half
     partner = col + 1 - 2 * parity
@@ -288,13 +294,14 @@
         return remote(cuts(square.at[low], low), cuts(mate, low), s_mate.at[0], r_mate.at[0], row, partner)
 
     other(trade, begin)
+    each(0, lines, settle)
     mine_or(trade, got)
     mine[...] = square[parity] + mate[...]
 
     def scatter(k):
         there = lax.rem(index + k, count)
         r, c = place(there)
-        return lambda low: remote(cut(mine.at[there], low), cut(piece.at[k], low), s_piece.at[k], r_piece.at[k], r, c)
+        return lambda low: remote(cut(mine.at[there], low), cut(piece.at[k], low), s_all.at[k], r_piece.at[k], r, c)
 
     each(1, count, lambda k: mine_or(scatter(k), begin))
     each(1, count, lambda k: mine_or(scatter(k), both))
@@ -304,14 +311,14 @@
 
     def collect(k):
         r, c = place(lax.rem(index + k, count))
-        return lambda low: remote(cut(done, low), cut(gram.at[parity, index], low), s_done.at[k], r_done.at[k], r, c)
+        return lambda low: remote(cut(done, low), cut(gram.at[parity, index], low), s_all.at[k], r_done.at[k], r, c)
 
     def pass_on(k):
         there = lax.rem(index + count - k, count)
 
         def make(low):
             ref = cut(gram.at[low, there], low)
-            return remote(ref, ref, s_over.at[k], r_over.at[k], row, partner)
+            return remote(ref, ref, s_all.at[count + k], r_over.at[k], row, partner)
 
         return make
 
@@ -320,7 +327,7 @@
         mine_or(pass_on(k), begin)
 
     def own(low):
-        return remote(cut(done, low), cut(gram.at[low, index], low), s_over.at[0], r_over.at[0], row, partner)
+        return remote(cut(done, low), cut(gram.at[low, index], low), s_all.at[count], r_over.at[0], row, partner)
 
     each(1, count, lambda k: mine_or(collect(k), begin))
     mine_or(own, begin)
@@ -349,7 +356,7 @@
     share = ranks // 2 // count
     f32 = jnp.float32
     dma = pltpu.SemaphoreType.DMA
-    wide = max(2, half)
+    wide, most = max(2, half), half - 1
     sample, gram = pl.pallas_call(
         functools.partial(sample_kernel, rows, cols),
         out_shape=(
@@ -368,11 +375,9 @@
             pltpu.VMEM((count, share, ranks), f32),
             pltpu.VMEM((count, share, ranks), f32),
             pltpu.VMEM((share, ranks), f32),
-            dma((2, 2, lines)), dma((2, lines)),
-            dma((2, lines, wide)), dma((2, lines, wide)),
-            dma((2, lines, wide, wide)), dma((2, lines, wide, wide)),
-            dma((2, lines, wide)), dma((2, lines, wide)),
-            dma((1,)), dma((1,)), dma((count,)), dma((count,)), dma((count,)), dma((count,)), dma((count,)), dma((count,)),
+            dma((max(2 * (lines + 1 + lines * most + lines * max(half, 2 * most) + lines * wide), 2 * count),)),
+            dma((2, lines)), dma((2, lines, most)), dma((2, lines, max(half, 2 * most))), dma((2, lines, wide)),
+            dma((1,)), dma((1,)), dma((count,)), dma((count,)), dma((count,)),
         ],
         compiler_params=pltpu.CompilerParams(
             collective_id=0,

time: 47.8 us -> 46.8 us (0.979)
  Pallas kernels: 46.3 us -> 45.3 us
    pallas_call x1, Pallas kernels: 38.8 us -> 37.8 us  [sketch_gram(): pl.pallas_call(functools.partial(sample_kernel, rows, cols), out_shape=(j...]
where the time goes in v5:
time: 46.8 us; the launch traced here: 46.6 us
  Pallas kernels  45.3 us (97%)
  between operations  1.28 us (3%)
    pallas_call x1, Pallas kernels, sketch_gram(): pl.pallas_call(functools.partial(sample_kernel, rows, cols), out_shape=(j...  37.8 us
    pallas_call x1, Pallas kernels, finish(): pl.pallas_call(functools.partial(finish_kernel, 1.0 / everyone), out_shap...  7.46 us

profile of v5, /device:TPU:0, one launch (start us, length us, event | category | flops | bytes accessed | tf_op | source)
XLA Modules:
  0.0 46.6 jit_solution(4114071961543903713)
XLA Ops:
  1.3 37.8 %sketch_gram.1 = (f32[160,256]{1,0:T(8,128)S(1)}, f32[2,16,8,256]{3,2,1,0:T(8,128)S(1)}) custom-call(f32[8,160]{1,0:T(8,128)} %points_hbm.1, bf16[160,256]{1,0:T(8,128)(2,1)} %tests.1, s32[1,160]{1,0:T(1,128)} %bitcast.3, s32[1]{0:T(128)S(6)} %copy.7.boundary, f32[8]{0:T(128)} %scales_hbm.1), custom_call_target="tpu_custom_call" | custom-call | tf_op jit(solution)/shard_map/sketch_gram/pallas_call | solution.py:360
  39.1 7.5 %finish.1 = (f32[160,256]{1,0:T(8,128)}, f32[256,256]{1,0:T(8,128)}) custom-call(f32[256,256]{1,0:T(8,128)S(1)} %bitcast.2, f32[160,256]{1,0:T(8,128)S(1)} %get-tuple-element.5.sample), custom_call_target="tpu_custom_call" | custom-call | tf_op jit(solution)/shard_map/finish/pallas_call | solution.py:499

commit v6 on v5

--- a/solution.py
+++ b/solution.py
@@ -144,17 +144,17 @@
     def leap(c, l, k):
         if c:
             return [
-                to_spot(back.at[l, spot, parity, (odd + k) % 2], j, send(2, 1, l * 2 * most + k * most + j - 1), r_b.at[1, l, k * most + j - 1])
+                to_spot(back.at[l, spot, parity, (odd + k) % 2], j, send(2, 1, l * 2 * most + k * most + j - 1), r_b.at[1, l])
                 for j in range(1, half)
             ]
-        return [to_mate(front.at[l, odd, parity, (spot + half - k) % half], send(2, 0, l * half + k), r_b.at[0, l, k])]
+        return [to_mate(front.at[l, odd, parity, (spot + half - k) % half], send(2, 0, l * half + k), r_b.at[0, l])]
 
     def leaps(c, l):
         return [copy for k in range(2 if c else half) for copy in leap(c, l, k)]
 
     def cross(c, l, j):
         ref = back.at[l, j, parity] if c else front.at[l, j, parity]
-        return remote(ref, ref, send(3, c, l * (half if c else 2) + j), r_c.at[c, l, j], *there(line, odd, spot, 1 - parity))
+        return remote(ref, ref, send(3, c, l * (half if c else 2) + j), r_c.at[c, l], *there(line, odd, spot, 1 - parity))
 
     def go(copies):
         for copy in copies:
@@ -211,11 +211,14 @@
             terms = [a + b for a, b in zip(terms[::2], terms[1::2])] + terms[len(terms) // 2 * 2 :]
         sample[...] += terms[0]
 
+    def landed(ref, recv):
+        remote(ref, ref, s_all.at[0], recv, row, col + 1 - 2 * parity).wait_recv()
+
     def close(n):
         l = origin(n)
-        come(leaps(0, l))
+        landed(front.at[l, 1 - odd, parity], r_b.at[0, l])
         cross(0, l, 1 - odd).start()
-        come(leaps(1, l))
+        landed(back.at[l, :most, parity], r_b.at[1, l])
         for k in range(1, half):
             cross(1, l, (spot + k) % half).start()
 
@@ -224,7 +227,8 @@
 
     def last(n):
         l = origin(n)
-        come([cross(0, l, j) for j in range(2)] + [cross(1, l, j) for j in range(half)])
+        landed(front.at[l, :, 1 - parity], r_c.at[0, l])
+        landed(back.at[l, :, 1 - parity], r_c.at[1, l])
         add(l, 1 - parity)
 
     def advance(n):
@@ -301,46 +305,37 @@
     def scatter(k):
         there = lax.rem(index + k, count)
         r, c = place(there)
-        return lambda low: remote(cut(mine.at[there], low), cut(piece.at[k], low), s_all.at[k], r_piece.at[k], r, c)
+        return lambda low: remote(cut(mine.at[there], low), cut(piece.at[k], low), s_all.at[k], r_piece.at[0], r, c)
 
     each(1, count, lambda k: mine_or(scatter(k), begin))
-    each(1, count, lambda k: mine_or(scatter(k), both))
+    def pieces(low):
+        ref = cuts(piece.at[1:], low)
+        return remote(ref, ref, s_all.at[0], r_piece.at[0], row, partner)
+
+    mine_or(pieces, got)
     piece[0] = mine[index]
     done[...] = jnp.sum(piece[...], axis=0)
     gram[parity, index] = done[...]
 
     def collect(k):
         r, c = place(lax.rem(index + k, count))
-        return lambda low: remote(cut(done, low), cut(gram.at[parity, index], low), s_all.at[k], r_done.at[k], r, c)
-
-    def pass_on(k):
-        there = lax.rem(index + count - k, count)
-
-        def make(low):
-            ref = cut(gram.at[low, there], low)
-            return remote(ref, ref, s_all.at[count + k], r_over.at[k], row, partner)
-
-        return make
-
-    def relay(k):
-        mine_or(collect(k), got)
-        mine_or(pass_on(k), begin)
-
-    def own(low):
-        return remote(cut(done, low), cut(gram.at[low, index], low), s_all.at[count], r_over.at[0], row, partner)
+        return lambda low: remote(cut(done, low), cut(gram.at[parity, index], low), s_all.at[count + k], r_done.at[0], r, c)
+
+    def rest(low):
+        ref = cuts(gram.at[low, 1:], low)
+        return remote(ref, ref, s_all.at[0], r_done.at[0], row, partner)
+
+    def pass_on(low):
+        ref = cuts(gram.at[low], low)
+        return remote(ref, ref, s_all.at[0], r_over.at[0], row, partner)
 
     each(1, count, lambda k: mine_or(collect(k), begin))
-    mine_or(own, begin)
-    each(1, count, relay)
-    mine_or(own, sent)
-    other(own, got)
-
-    def last_waits(k):
-        mine_or(pass_on(k), sent)
-        other(pass_on(k), got)
-        mine_or(collect(k), sent)
-
-    each(1, count, last_waits)
+    each(1, count, lambda k: mine_or(scatter(k), sent))
+    mine_or(rest, got)
+    mine_or(pass_on, begin)
+    each(1, count, lambda k: mine_or(collect(k), sent))
+    mine_or(pass_on, sent)
+    other(pass_on, got)
     other(trade, sent)
 
 
@@ -376,8 +371,8 @@
             pltpu.VMEM((count, share, ranks), f32),
             pltpu.VMEM((share, ranks), f32),
             dma((max(2 * (lines + 1 + lines * most + lines * max(half, 2 * most) + lines * wide), 2 * count),)),
-            dma((2, lines)), dma((2, lines, most)), dma((2, lines, max(half, 2 * most))), dma((2, lines, wide)),
-            dma((1,)), dma((1,)), dma((count,)), dma((count,)), dma((count,)),
+            dma((2, lines)), dma((2, lines, most)), dma((2, lines)), dma((2, lines)),
+            dma((1,)), dma((1,)), dma((1,)), dma((1,)), dma((1,)),
         ],
         compiler_params=pltpu.CompilerParams(
             collective_id=0,

time: 46.8 us -> 46.2 us (0.987)
  Pallas kernels: 45.3 us -> 44.7 us
    pallas_call x1, Pallas kernels: 37.8 us -> 37.3 us  [sketch_gram(): pl.pallas_call(functools.partial(sample_kernel, rows, cols), out_shape=(j...]
where the time goes in v6:
time: 46.2 us; the launch traced here: 46 us
  Pallas kernels  44.7 us (97%)
  between operations  1.28 us (3%)
    pallas_call x1, Pallas kernels, sketch_gram(): pl.pallas_call(functools.partial(sample_kernel, rows, cols), out_shape=(j...  37.3 us
    pallas_call x1, Pallas kernels, finish(): pl.pallas_call(functools.partial(finish_kernel, 1.0 / everyone), out_shap...  7.46 us

profile of v6, /device:TPU:0, one launch (start us, length us, event | category | flops | bytes accessed | tf_op | source)
XLA Modules:
  0.0 46.0 jit_solution(13240367879903486357)
XLA Ops:
  1.3 37.3 %sketch_gram.1 = (f32[160,256]{1,0:T(8,128)S(1)}, f32[2,16,8,256]{3,2,1,0:T(8,128)S(1)}) custom-call(f32[8,160]{1,0:T(8,128)} %points_hbm.1, bf16[160,256]{1,0:T(8,128)(2,1)} %tests.1, s32[1,160]{1,0:T(1,128)} %bitcast.3, s32[1]{0:T(128)S(6)} %copy.7.boundary, f32[8]{0:T(128)} %scales_hbm.1), custom_call_target="tpu_custom_call" | custom-call | tf_op jit(solution)/shard_map/sketch_gram/pallas_call | solution.py:355
  38.6 7.5 %finish.1 = (f32[160,256]{1,0:T(8,128)}, f32[256,256]{1,0:T(8,128)}) custom-call(f32[256,256]{1,0:T(8,128)S(1)} %bitcast.2, f32[160,256]{1,0:T(8,128)S(1)} %get-tuple-element.5.sample), custom_call_target="tpu_custom_call" | custom-call | tf_op jit(solution)/shard_map/finish/pallas_call | solution.py:494

commit v7 on v6

--- a/solution.py
+++ b/solution.py
@@ -197,16 +197,19 @@
                 go(leap(c, l, k))
             cross(c, l, spot if c else odd).start()
 
-    def add(l, p):
+    def add(l, p, gate=None):
+        places = [(o, s) for o in range(2) for s in range(half)]
+        tiles = []
+        for o, s in places:
+            head, foot = front[l, o, p, s, split : split + 16, :local], front[l, o, p, s, split + 16 :, :local]
+            right = jnp.concatenate([head, head, head, foot], axis=0)
+            tiles.append(jnp.exp(dot(left[...], right, ((1,), (0,)), None)).astype(jnp.bfloat16))
+        if gate:
+            gate()
         terms = []
-        for o in range(2):
-            for s in range(half):
-                pack = front[l, o, p, s]
-                body, head, foot = pack[:split], pack[split : split + 16, :local], pack[split + 16 :, :local]
-                right = jnp.concatenate([head, head, head, foot], axis=0)
-                tile = jnp.exp(dot(left[...], right, ((1,), (0,)), None)).astype(jnp.bfloat16)
-                test = jnp.concatenate([body, back[l, s, p, o]], axis=0)
-                terms.append(dot(tile, test, ((1,), (0,)), None))
+        for (o, s), tile in zip(places, tiles):
+            test = jnp.concatenate([front[l, o, p, s, :split], back[l, s, p, o]], axis=0)
+            terms.append(dot(tile, test, ((1,), (0,)), None))
         while len(terms) > 1:
             terms = [a + b for a, b in zip(terms[::2], terms[1::2])] + terms[len(terms) // 2 * 2 :]
         sample[...] += terms[0]
@@ -228,8 +231,7 @@
     def last(n):
         l = origin(n)
         landed(front.at[l, :, 1 - parity], r_c.at[0, l])
-        landed(back.at[l, :, 1 - parity], r_c.at[1, l])
-        add(l, 1 - parity)
+        add(l, 1 - parity, lambda: landed(back.at[l, :, 1 - parity], r_c.at[1, l]))
 
     def advance(n):
         arrive(n + 1)
@@ -292,15 +294,18 @@
     def both(copy):
         copy.wait()
 
-    square[...] = product(total, total, ((0,), (0,))).reshape(square.shape)
+    first, second = total[:, : ranks // 2], total[:, ranks // 2 :]
+    square[...] = product(jnp.where(parity == 0, second, first), total, ((0,), (0,))).reshape(square.shape)
 
     def trade(low):
-        return remote(cuts(square.at[low], low), cuts(mate, low), s_mate.at[0], r_mate.at[0], row, partner)
+        return remote(cuts(square, low), cuts(mate, low), s_mate.at[0], r_mate.at[0], row, partner)
 
     other(trade, begin)
+    kept = product(jnp.where(parity == 0, first, second), total, ((0,), (0,))).reshape(square.shape)
+    mine[...] = kept
     each(0, lines, settle)
     mine_or(trade, got)
-    mine[...] = square[parity] + mate[...]
+    mine[...] = mine[...] + mate[...]
 
     def scatter(k):
         there = lax.rem(index + k, count)
@@ -365,7 +370,7 @@
             pltpu.VMEM((lines, half, 2, 2, local - split, ranks), tests.dtype),
             pltpu.VMEM((local, 2 * lanes), tests.dtype),
             pltpu.VMEM(points.shape, f32), pltpu.VMEM((1, local), rank.dtype), pltpu.SMEM(scales.shape, f32), dma((5,)),
-            pltpu.VMEM((2, count, share, ranks), f32),
+            pltpu.VMEM((count, share, ranks), f32),
             pltpu.VMEM((count, share, ranks), f32),
             pltpu.VMEM((count, share, ranks), f32),
             pltpu.VMEM((count, share, ranks), f32),

time: 46.2 us -> 46.2 us (level)
  no operation moved by 1% of the time
where the time goes in v7:
time: 46.2 us; the launch traced here: 46 us
  Pallas kernels  44.7 us (97%)
  between operations  1.28 us (3%)
    pallas_call x1, Pallas kernels, sketch_gram(): pl.pallas_call(functools.partial(sample_kernel, rows, cols), out_shape=(j...  37.2 us
    pallas_call x1, Pallas kernels, finish(): pl.pallas_call(functools.partial(finish_kernel, 1.0 / everyone), out_shap...  7.46 us

profile of v7, /device:TPU:0, one launch (start us, length us, event | category | flops | bytes accessed | tf_op | source)
XLA Modules:
  0.0 46.0 jit_solution(10676697775743653886)
XLA Ops:
  1.3 37.2 %sketch_gram.1 = (f32[160,256]{1,0:T(8,128)S(1)}, f32[2,16,8,256]{3,2,1,0:T(8,128)S(1)}) custom-call(f32[8,160]{1,0:T(8,128)} %points_hbm.1, bf16[160,256]{1,0:T(8,128)(2,1)} %tests.1, s32[1,160]{1,0:T(1,128)} %bitcast.3, s32[1]{0:T(128)S(6)} %copy.7.boundary, f32[8]{0:T(128)} %scales_hbm.1), custom_call_target="tpu_custom_call" | custom-call | tf_op jit(solution)/shard_map/sketch_gram/pallas_call | solution.py:360
  38.5 7.5 %finish.1 = (f32[160,256]{1,0:T(8,128)}, f32[256,256]{1,0:T(8,128)}) custom-call(f32[256,256]{1,0:T(8,128)S(1)} %bitcast.2, f32[160,256]{1,0:T(8,128)S(1)} %get-tuple-element.5.sample), custom_call_target="tpu_custom_call" | custom-call | tf_op jit(solution)/shard_map/finish/pallas_call | solution.py:499
